TPU v7x, 256 devices: a whole 4x4x8 slice. The times are simulated.
256 devices in a mesh: grp: 8 (over x, core), dev: 32 (over z, y).
Axes of the slice: x: 4, y: 4, z: 8, core: 2. Of those that a mesh axis runs over, the one named last changes fastest.
Arguments:
- ladder_amps: bfloat16 [64, 144, 4096], P('dev', 'grp'), may hold values from -6 to 6
- ladder_ids: int32 [64, 144], P('dev', 'grp'), may hold values from 0 to 23, as said below
- ladder_count: int32 [64, 8], P('dev', 'grp'), may hold values from 9 to 18, as said below
- cycle_amps: bfloat16 [64, 48, 4096], P('dev', 'grp'), may hold values from -6 to 6
- cycle_ids: int32 [64, 48], P('dev', 'grp'), may hold values from 0 to 7, as said below
- cycle_count: int32 [64, 8], P('dev', 'grp'), may hold values from 3 to 6, as said below
- ladder_panel: bfloat16 [12288, 16384], P('grp', 'dev'), may hold values from -0.0546875 to 0.0546875
- cycle_panel: bfloat16 [4096, 16384], P('grp', 'dev'), may hold values from -0.09375 to 0.09375
- owners: int32 [64], replicated, may hold values from 0 to 63, each once
- base: float32 [4096, 16384], P('grp', 'dev'), may hold values from -6 to 6
Outputs:
- residual: float32 [4096, 16384], P('grp', 'dev')
Inputs may be any that keep to these rules, and one draw needn't show every extreme that they name: `ladder_ids`: within one row tile and group the slots name distinct tiles of 0 to 23. `cycle_ids`: within one row tile and group the slots name distinct tiles of 0 to 7. `ladder_count`: slots at or past the count are not live; in every group some row tile has all 18 slots live. `cycle_count`: slots at or past the count are not live; in every group some row tile has all 6 slots live.
All inputs are finite; a program needn't handle non-finite values.
Results may differ from a plain program's by a relative error of at most 0.0003.
Values may be sent and summed in bfloat16 or wider, within the bound.
A program may use at most 128 MiB of HBM per device.

v0:
```python
import jax
import jax.numpy as jnp
from jax import lax
from jax.sharding import PartitionSpec as P

TS = 64
KLT = 24
KRT = 8


def in_one_piece(arrays, axis, dim, along):
    ends, at = ([], 0)
    for a in arrays[:-1]:
        at += a.shape[along]
        ends.append(at)
    both = jnp.concatenate(arrays, axis=along)
    return tuple(jnp.split(lax.all_gather(both, axis, axis=dim, tiled=True), ends, axis=along))


def live_mask(ids, count):
    slots = ids.shape[1]
    return (jnp.arange(slots, dtype=jnp.int32)[None, :] < count).astype(jnp.bfloat16)


def place_tiles(amps, ids, count, ktiles):
    tile_rows, slots = ids.shape
    onehot = (ids[:, :, None] == jnp.arange(ktiles, dtype=jnp.int32)[None, None, :]).astype(
        jnp.bfloat16
    )
    onehot = onehot * live_mask(ids, count)[:, :, None]
    tiles = amps.reshape(tile_rows, slots, TS, TS)
    dense = jnp.einsum("rjk,rjab->rakb", onehot, tiles, preferred_element_type=jnp.float32)
    return dense.astype(jnp.bfloat16).reshape(tile_rows * TS, ktiles * TS)


def per_device(
    ladder_amps,
    ladder_ids,
    ladder_count,
    cycle_amps,
    cycle_ids,
    cycle_count,
    ladder_panel,
    cycle_panel,
    owners,
    base,
):
    own_ladder = place_tiles(ladder_amps, ladder_ids, ladder_count, KLT)
    own_cycle = place_tiles(cycle_amps, cycle_ids, cycle_count, KRT)
    all_ladder, all_cycle = in_one_piece((own_ladder, own_cycle), "dev", 0, 1)
    count = base.shape[0] * lax.axis_size("grp")
    ladder_rows = all_ladder.reshape(-1, TS, KLT * TS)[owners].reshape(count, KLT * TS)
    cycle_rows = all_cycle.reshape(-1, TS, KRT * TS)[owners].reshape(count, KRT * TS)
    result = jnp.dot(ladder_rows, ladder_panel, preferred_element_type=jnp.float32)
    summed = lax.psum_scatter(
        result + jnp.dot(cycle_rows, cycle_panel, preferred_element_type=jnp.float32),
        "grp",
        scatter_dimension=0,
        tiled=True,
    )
    return base + summed


def solution(mesh):
    placed = (
        P("dev", "grp", None),
        P("dev", "grp"),
        P("dev", "grp"),
        P("dev", "grp", None),
        P("dev", "grp"),
        P("dev", "grp"),
        P("grp", "dev"),
        P("grp", "dev"),
        P(),
        P("grp", "dev"),
    )
    return jax.shard_map(
        per_device, mesh=mesh, in_specs=placed, out_specs=P("grp", "dev"), check_vma=False
    )
```

profile of v0, /device:TPU:1, one launch (start us, length us, event | category | flops | bytes accessed | tf_op | source)
XLA Modules:
  0.0 266.0 jit_solution(7264892587151928912)
XLA Ops:
  6.5 0.0 copy-start
  6.5 0.0 all-gather.2.cloned.1.call-start
  6.5 0.8 compare_convert_fusion.1
  7.4 0.7 compare_convert_fusion
  8.1 1.1 reshape.74
  9.2 0.9 fusion.1
  10.1 0.2 reshape.75
  10.3 1.4 reshape.72
  11.7 1.3 fusion
  13.0 0.5 reshape.73
  13.5 0.9 pad_maximum_fusion
  14.3 0.0 all-gather.2.cloned.1.call-update
  14.3 0.0 reduce-scatter.2.cloned.1.call-start
  14.4 0.7 compare_select_fusion
  15.1 142.2 %all-gather.2.cloned.1.call-done = bf16[4096,2048]{1,0:T(8,128)(2,1)} async-done(((bf16[128,2048]{1,0:T(8,128)(2,1)}), bf16[4096,2048]{1,0:T(8,128)(2,1)}) %all-gather.2.cloned.1.call-update) | async-done | bytes 16777232 | tf_op jit(solution)/shard_map/all_gather | solution.py:17
  157.3 10.4 %split.8 = bf16[4096,1536]{1,0:T(8,128)(2,1)} slice(bf16[4096,2048]{1,0:T(8,128)(2,1)} %all-gather.2.cloned.1.call-done), slice={[0:4096], [0:1536]} | slice | bytes 25165824 | tf_op jit(solution)/shard_map/split | solution.py:17
  167.7 11.9 %gather_fusion = bf16[64,64,1536]{2,1,0:T(8,128)(2,1)} fusion(bf16[64,64,1536]{2,1,0:T(8,128)(2,1)} %bitcast.32, s32[1024]{0:T(1024)S(1)} %pad_clamp_fusion), kind=kCustom, calls=%fused_computation | custom fusion | bytes 25166080 | tf_op jit(solution)/shard_map/gather | solution.py:52
  179.6 0.0 copy-start.3
  179.6 4.4 %split.9 = bf16[4096,512]{1,0:T(8,128)(2,1)} slice(bf16[4096,2048]{1,0:T(8,128)(2,1)} %all-gather.2.cloned.1.call-done), slice={[0:4096], [1536:2048]} | slice | bytes 8388608 | tf_op jit(solution)/shard_map/split | solution.py:17
  184.0 4.9 %gather_fusion.1 = bf16[64,64,512]{2,1,0:T(8,128)(2,1)} fusion(bf16[64,64,512]{2,1,0:T(8,128)(2,1)} %bitcast.34, s32[1024]{0:T(1024)S(1)} %pad_clamp_fusion), kind=kCustom, calls=%fused_computation.1 | custom fusion | bytes 8388864 | tf_op jit(solution)/shard_map/gather | solution.py:53
  189.0 0.0 copy-start.1
  189.0 0.0 copy-done.3
  189.0 4.8 %fusion.18 = f32[4096,512]{1,0:T(8,128)S(1)} fusion(bf16[4096,512]{1,0:T(8,128)(2,1)} %bitcast.33, bf16[512,512]{1,0:T(8,128)(2,1)S(1)} %copy-done.3), kind=kOutput, calls=%fused_computation.28 | convolution fusion | flops 2147483648 | bytes 13107200 | tf_op jit(solution)/shard_map/dot_general | solution.py:56
  193.7 0.0 copy-done
  193.7 1.1 copy-done.1
  194.8 9.5 %convolution_add_fusion = f32[4096,512]{1,0:T(8,128)} fusion(f32[4096,512]{1,0:T(8,128)S(1)} %fusion.18, bf16[4096,1536]{1,0:T(8,128)(2,1)S(1)} %bitcast.35, bf16[1536,512]{1,0:T(8,128)(2,1)S(1)} %copy-done), kind=kOutput, calls=%fused_computation.2 | convolution fusion | flops 6444548096 | bytes 30932992 | tf_op jit(solution)/shard_map/dot_general | solution.py:54
  204.3 0.0 copy-start.2
  204.3 0.0 reduce-scatter.2.cloned.1.call-update
  204.3 52.4 %reduce-scatter.2.cloned.1.call-done = f32[512,512]{1,0:T(8,128)} async-done(((f32[4096,512]{1,0:T(8,128)}), f32[512,512]{1,0:T(8,128)}) %reduce-scatter.2.cloned.1.call-update) | async-done | bytes 1048592 | tf_op jit(solution)/shard_map/reduce_scatter | solution.py:55
  256.7 0.0 copy-done.2
  256.7 2.4 add.14
  (1 shorter events, 0.0 us)
Async XLA Ops:
  6.5 187.2 %copy-start = (bf16[1536,512]{1,0:T(8,128)(2,1)S(1)}, bf16[1536,512]{1,0:T(8,128)(2,1)}, u32[]{:S(2)}) copy-start(bf16[1536,512]{1,0:T(8,128)(2,1)} %param.16) | copy-start | bytes 4718596
  6.5 150.7 %all-gather.2.cloned.1.call-start = ((), (), s32[]{:S(2)}) async-start(), calls=%async_computation.1 | async-start | bytes 17301504 | tf_op jit(solution)/shard_map/all_gather | solution.py:17
  14.3 242.4 %reduce-scatter.2.cloned.1.call-start = ((), (), s32[]{:S(2)}) async-start(), calls=%async_computation.2 | async-start | bytes 9437184 | tf_op jit(solution)/shard_map/reduce_scatter | solution.py:55
  179.6 9.4 %copy-start.3 = (bf16[512,512]{1,0:T(8,128)(2,1)S(1)}, bf16[512,512]{1,0:T(8,128)(2,1)}, u32[]{:S(2)}) copy-start(bf16[512,512]{1,0:T(8,128)(2,1)} %param.17) | copy-start | bytes 1572868
  189.0 5.8 %copy-start.1 = (bf16[64,64,1536]{2,1,0:T(8,128)(2,1)S(1)}, bf16[64,64,1536]{2,1,0:T(8,128)(2,1)}, u32[]{:S(2)}) copy-start(bf16[64,64,1536]{2,1,0:T(8,128)(2,1)} %gather_fusion) | copy-start | bytes 37748740
  204.3 52.4 %copy-start.2 = (f32[512,512]{1,0:T(8,128)S(1)}, f32[512,512]{1,0:T(8,128)}, u32[]{:S(2)}) copy-start(f32[512,512]{1,0:T(8,128)} %param.19) | copy-start | bytes 3145732
Sparse Core Ops, SparseCore 0:
  14.5 142.7 all-gather.1
  204.4 52.2 reduce-scatter.1
where the time goes:
time: 266 us
  waiting for transfers between devices  195 us (73%)
  local copies, waits for them, and re-layouts  35.9 us (13%)
  matrix products  16.4 us (6%)
  between operations  13.4 us (5%)
  other arithmetic  5.49 us (2%)
    all_gather x1, waiting for transfers between devices, in_one_piece(): lax.all_gather(both, axis, axis=dim, tiled=True)  142 us
    reduce_scatter x1, waiting for transfers between devices, per_device(): lax.psum_scatter(result + jnp.dot(cycle_rows, cycle_panel, preferred_elem...  52.4 us
    split x2, local copies, waits for them, and re-layouts, in_one_piece(): jnp.split(lax.all_gather(both, axis, axis=dim, tiled=True), ends, axis=al...  14.9 us
    gather x1, local copies, waits for them, and re-layouts, per_device(): all_ladder.reshape(-1, TS, KLT * TS)[owners].reshape(count, KLT * TS)  11.9 us
    dot_general x1, matrix products, per_device(): jnp.dot(ladder_rows, ladder_panel, preferred_element_type=jnp.float32)  9.48 us
  transfers between devices with their start and end apart: 2, of which 2 were waited for; matrix products, arithmetic and copies ran while one was open for 0% of the time, Pallas kernels for 0%

commit v1 on v0

v1 whole, which is shorter than its diff:
```python
import jax
import jax.numpy as jnp
from jax import lax
from jax.experimental import pallas as pl
from jax.experimental.pallas import tpu as pltpu
from jax.sharding import PartitionSpec as P

TS = 64
KLT = 24
KRT = 8
MESH = pl.DeviceIdType.MESH
STEPS = 16
PAIRS = 12
HALF = 32
ZERO = PAIRS
VAR = PAIRS + 1


def pos_first(z, y):
    return 4 * z + (y + z) % 4


def dev_first(s):
    k = s // 4
    return 4 * k + (s % 4 + 32 - k) % 4


def pos_second(z, y):
    t = (z + 24 - 3 * y) % 8
    return 4 * y + 16 * (t // 4) + t % 4


def dev_second(s):
    k = s // 4
    return 4 * ((3 * k + s % 4) % 8) + k % 4


POS = (pos_first, pos_second)
DEV = (dev_first, dev_second)


def kernel(
    own, tab_in, loc, lad, cyc, out,
    held, tab_v, tab_s, panel, spread, lhs, part, got, total, fin_s, fin_r,
    local_sem, pair_s, pair_r, tab_ss, tab_rs, ring_s, ring_r, red_s, red_r, sh_s, sh_r, fin_ss, fin_rs,
):
    g = lax.axis_index("grp")
    d = lax.axis_index("dev")
    x = g // 2
    c = g % 2
    z = d // 4
    y = d % 4
    other = 1 - c
    mate = (2 * x + other, d)
    pos = [POS[h](z, y) for h in range(2)]
    nxt = [(g, DEV[h]((pos[h] + 1) % 32)) for h in range(2)]
    prv = [(g, DEV[h]((pos[h] + 31) % 32)) for h in range(2)]

    def local(i, src, dst):
        return pltpu.make_async_copy(src, dst, local_sem.at[i])

    def to_mate(i, src, dst):
        return pltpu.make_async_remote_copy(
            src_ref=src, dst_ref=dst, send_sem=pair_s.at[i], recv_sem=pair_r.at[i],
            device_id=mate, device_id_type=MESH)

    locals_ = [
        local(0, own.at[c, 0], held.at[0, 0, c]),
        local(1, own.at[c, 1], held.at[1, 0, c]),
        local(2, tab_in.at[c], tab_v.at[d, c]),
        local(3, lad, panel.at[c, pl.ds(0, 1536)]),
        local(4, cyc, panel.at[c, pl.ds(1536, 512)]),
    ]

    def mates(side):
        return [
            to_mate(0, own.at[other, 0], held.at[0, 0, side]),
            to_mate(1, own.at[other, 1], held.at[1, 0, side]),
            to_mate(2, tab_in.at[other], tab_v.at[d, side]),
            to_mate(3, lad, panel.at[side, pl.ds(0, 1536)]),
            to_mate(4, cyc, panel.at[side, pl.ds(1536, 512)]),
        ]

    going = mates(c)
    coming = mates(other)
    for i in range(5):
        locals_[i].start()
        going[i].start()

    def hop(h, up, src, dst, kg):
        return pltpu.make_async_remote_copy(
            src_ref=held.at[h, src, kg], dst_ref=held.at[h, dst, kg],
            send_sem=ring_s.at[h, dst, kg], recv_sem=ring_r.at[h, dst, kg],
            device_id=nxt[h] if up else prv[h], device_id_type=MESH)

    for h in range(2):
        locals_[h].wait()
    for h in range(2):
        coming[h].wait_recv()
    for kg in range(2):
        for h in range(2):
            hop(h, True, 0, 1, kg).start()
            hop(h, False, 0, 31, kg).start()

    locals_[2].wait()
    coming[2].wait_recv()

    def table_to(i):
        return pltpu.make_async_remote_copy(
            src_ref=tab_v.at[d], dst_ref=tab_v.at[d], send_sem=tab_ss, recv_sem=tab_rs,
            device_id=(g, (d + i) % 32), device_id_type=MESH)

    @pl.loop(1, 32)
    def _(i):
        table_to(i).start()

    spread[ZERO] = jnp.zeros((HALF, 128), jnp.bfloat16)
    spread[VAR + ZERO] = jnp.zeros((HALF, 128), jnp.bfloat16)

    every = tab_v.at[pl.ds(0, 31)]
    pltpu.make_async_copy(every, every, tab_rs).wait()
    pltpu.make_async_copy(every, every, tab_ss).wait()
    to_smem = pltpu.make_async_copy(tab_v, tab_s, local_sem.at[5])
    to_smem.start()
    for i in (3, 4):
        locals_[i].wait()
        coming[i].wait_recv()
    to_smem.wait()

    left = lax.broadcasted_iota(jnp.int32, (HALF, 128), 1) < 64

    def reduce_copy(b, r):
        to = (x + r) % 4
        return pltpu.make_async_remote_copy(
            src_ref=part.at[b, to], dst_ref=got.at[b, r - 1],
            send_sem=red_s.at[b, r - 1], recv_sem=red_r.at[b, r - 1],
            device_id=(2 * to + c, d), device_id_type=MESH)

    def share_copy(b, side):
        rows = total.at[pl.ds((side * STEPS + b) * 4, 4)]
        return pltpu.make_async_remote_copy(
            src_ref=rows, dst_ref=rows, send_sem=sh_s.at[b], recv_sem=sh_r.at[b],
            device_id=mate, device_id_type=MESH)

    def finish(b):
        for r in (1, 2, 3):
            reduce_copy(b, r).wait_recv()
        s = part[b, x] + got[b, 0] + got[b, 1] + got[b, 2]
        for q in range(4):
            total[(c * STEPS + b) * 4 + q] = s[HALF * q:HALF * (q + 1)]
        share_copy(b, c).start()

    @pl.loop(0, STEPS)
    def _(b):
        for kg in range(2):
            for h in range(2):
                @pl.when(b < 15)
                def _():
                    hop(h, True, b, b + 1, kg).wait_recv()

                @pl.when(b < 14)
                def _():
                    hop(h, True, b + 1, b + 2, kg).start()

                hop(h, False, 0, 31 - b, kg).wait_recv()

                @pl.when(b < 15)
                def _():
                    hop(h, False, 31 - b, 30 - b, kg).start()

            for q in range(4):
                h = q // 2
                m = b if q % 2 == 0 else 31 - b
                src = DEV[h]((pos[h] + 32 - m) % 32)
                for p in range(PAIRS):
                    v = held[h, m, kg, p]
                    spread[p] = v
                    spread[VAR + p] = jnp.concatenate([v[:, 64:], v[:, :64]], axis=1)
                for j in range(16):
                    a = tab_s[src, kg, 0, 2 * j]
                    e = tab_s[src, kg, 0, 2 * j + 1]
                    lhs[HALF * q:HALF * (q + 1), 128 * j:128 * (j + 1)] = jnp.where(left, spread[a], spread[e])
            prod = jnp.dot(lhs[...], panel[kg], preferred_element_type=jnp.float32)
            for q in range(4):
                piece = prod[:, 128 * q:128 * (q + 1)]
                part[b, q] = piece if kg == 0 else part[b, q] + piece
        for r in (2, 1, 3):
            reduce_copy(b, r).start()

        @pl.when(b >= 2)
        def _():
            finish(b - 2)

    finish(STEPS - 2)
    finish(STEPS - 1)

    @pl.loop(0, STEPS)
    def _(b):
        share_copy(b, other).wait_recv()

    def final_copy(r):
        to = (x + r) % 4
        return pltpu.make_async_remote_copy(
            src_ref=fin_s.at[r], dst_ref=fin_r.at[r - 1], send_sem=fin_ss.at[r - 1], recv_sem=fin_rs.at[r - 1],
            device_id=(2 * to + c, d), device_id_type=MESH)

    for r in (2, 1, 3, 0):
        to = (x + r) % 4
        for i in range(16):
            fin_s[r, HALF * i:HALF * (i + 1)] = total[loc[to * 16 + i]]
        if r:
            final_copy(r).start()
    out[x] = fin_s[0]
    for r in (1, 3, 2):
        final_copy(r).wait_recv()
        out[(x + 4 - r) % 4] = fin_r[r - 1]

    for i in range(5):
        going[i].wait_send()
    for r in (1, 2, 3):
        final_copy(r).wait_send()

    @pl.loop(0, STEPS)
    def _(b):
        share_copy(b, c).wait_send()
        for r in (1, 2, 3):
            reduce_copy(b, r).wait_send()
        for kg in range(2):
            for h in range(2):
                @pl.when(b < 15)
                def _():
                    hop(h, True, b, b + 1, kg).wait_send()
                hop(h, False, 0, 31 - b, kg).wait_send()


def per_device(
    ladder_amps, ladder_ids, ladder_count, cycle_amps, cycle_ids, cycle_count,
    ladder_panel, cycle_panel, owners, base,
):
    i32 = jnp.int32
    amps = jnp.concatenate([ladder_amps, cycle_amps], axis=1)
    own = amps.reshape(2, PAIRS, 2, 2, HALF, TS).transpose(0, 3, 1, 4, 2, 5).reshape(2, 2, PAIRS, HALF, 128)

    ids = jnp.concatenate([ladder_ids, cycle_ids + KLT], axis=1)
    nl, nc = ladder_ids.shape[1], cycle_ids.shape[1]
    slot = jnp.arange(nl + nc, dtype=i32)
    live = jnp.where(slot < nl, slot[None] < ladder_count, slot[None] - nl < cycle_count)
    code = VAR * ((slot & 1)[None] ^ (ids & 1)) + (slot // 2)[None] - ZERO
    hit = (ids[:, :, None] == jnp.arange(128, dtype=i32)) & live[:, :, None]
    table = ZERO + jnp.sum(jnp.where(hit, code[:, :, None], 0), axis=1, dtype=i32)
    table = table.reshape(2, 1, 128)

    g = lax.axis_index("grp")
    d = lax.axis_index("dev")
    c, z, y = g % 2, d // 4, d % 4
    tiles = owners.reshape(4, 2, 8)[:, c]
    src = tiles // 2
    spots = []
    for h in range(2):
        m = (POS[h](z, y) + 32 - POS[h](src // 4, src % 4)) % 32
        far = (m >= STEPS).astype(i32)
        b = jnp.where(m >= STEPS, 31 - m, m)
        spots.append((tiles % 2 * STEPS + b) * 4 + 2 * h + far)
    loc = jnp.stack(spots, axis=-1).reshape(64)

    hbm = pl.BlockSpec(memory_space=pl.ANY)
    bf16, f32 = jnp.bfloat16, jnp.float32
    dma = pltpu.SemaphoreType.DMA
    summed = pl.pallas_call(
        kernel,
        name="ladder_ring",
        out_shape=jax.ShapeDtypeStruct((4, 512, 128), f32),
        in_specs=[hbm, hbm, pl.BlockSpec(memory_space=pltpu.SMEM), hbm, hbm],
        out_specs=pl.BlockSpec(memory_space=pltpu.VMEM),
        scratch_shapes=[
            pltpu.VMEM((2, 32, 2, PAIRS, HALF, 128), bf16),
            pltpu.VMEM((32, 2, 1, 128), i32),
            pltpu.SMEM((32, 2, 1, 128), i32),
            pltpu.VMEM((2, 2048, 512), bf16),
            pltpu.VMEM((2 * VAR, HALF, 128), bf16),
            pltpu.VMEM((128, 2048), bf16),
            pltpu.VMEM((STEPS, 4, 128, 128), f32),
            pltpu.VMEM((STEPS, 3, 128, 128), f32),
            pltpu.VMEM((2 * STEPS * 4, HALF, 128), f32),
            pltpu.VMEM((4, 512, 128), f32),
            pltpu.VMEM((3, 512, 128), f32),
            dma((6,)), dma((5,)), dma((5,)), dma, dma,
            dma((2, 32, 2)), dma((2, 32, 2)),
            dma((STEPS, 3)), dma((STEPS, 3)), dma((STEPS,)), dma((STEPS,)),
            dma((3,)), dma((3,)),
        ],
        compiler_params=pltpu.CompilerParams(has_side_effects=True, vmem_limit_bytes=58 * 2**20),
    )(own, table, loc, ladder_panel, cycle_panel)
    return base + summed.transpose(1, 0, 2).reshape(512, 512)


def solution(mesh):
    placed = (
        P("dev", "grp", None),
        P("dev", "grp"),
        P("dev", "grp"),
        P("dev", "grp", None),
        P("dev", "grp"),
        P("dev", "grp"),
        P("grp", "dev"),
        P("grp", "dev"),
        P(),
        P("grp", "dev"),
    )
    return jax.shard_map(
        per_device, mesh=mesh, in_specs=placed, out_specs=P("grp", "dev"), check_vma=False
    )
```

time: 266 us -> 139 us (0.52)
  waiting for transfers between devices: 195 us -> 0 us
  Pallas kernels: 0 us -> 127 us
  local copies, waits for them, and re-layouts: 35.9 us -> 7.22 us
  matrix products: 16.4 us -> 0 us
  between operations: 13.4 us -> 0.08 us
    all_gather x1 -> x0, waiting for transfers between devices: 142 us -> none  [in_one_piece(): lax.all_gather(both, axis, axis=dim, tiled=True)]
    pallas_call x0 -> x1, Pallas kernels: none -> 127 us  [per_device(): pl.pallas_call(kernel, name='ladder_ring', out_shape=jax.ShapeDtypeStruct...]
    reduce_scatter x1 -> x0, waiting for transfers between devices: 52.4 us -> none  [per_device(): lax.psum_scatter(result + jnp.dot(cycle_rows, cycle_panel, preferred_elem...]
    gather x2 -> x0, local copies, waits for them, and re-layouts: 16.8 us -> none  [the longest x1 11.9 us: per_device(): all_ladder.reshape(-1, TS, KLT * TS)[owners].reshape(count, KLT * TS)]
    dot_general x4 -> x0, matrix products: 16.4 us -> none  [the longest x1 9.48 us: per_device(): jnp.dot(ladder_rows, ladder_panel, preferred_element_type=jnp.float32)]
    split x2 -> x0, local copies, waits for them, and re-layouts: 14.9 us -> none  [in_one_piece(): jnp.split(lax.all_gather(both, axis, axis=dim, tiled=True), ends, axis=al...]
  transfers between devices with their start and end apart: 2 -> 0, of which waited for: 2 -> 0; matrix products, arithmetic and copies ran while one was open for 0% -> 0% of each run, Pallas kernels for 0% -> 0%
where the time goes in v1:
time: 139 us
  Pallas kernels  127 us (91%)
  local copies, waits for them, and re-layouts  7.22 us (5%)
  other arithmetic  4.68 us (3%)
    pallas_call x1, Pallas kernels, per_device(): pl.pallas_call(kernel, name='ladder_ring', out_shape=jax.ShapeDtypeStruct...  127 us

profile of v1, /device:TPU:1, one launch (start us, length us, event | category | flops | bytes accessed | tf_op | source)
XLA Modules:
  0.0 139.1 jit_solution(316862836830292677)
XLA Ops:
  0.0 0.7 compare_select_fusion
  0.8 0.7 broadcast_add_fusion.1
  1.4 0.8 add_add_fusion
  2.2 0.1 select_reduce_fusion
  2.3 0.6 broadcast_add_fusion
  2.9 0.7 reshape.608
  3.6 0.1 fusion.1
  3.7 0.1 copy.19
  3.8 0.7 reshape.609.loc
  4.5 1.5 %pad_maximum_fusion = bf16[2,24,4096]{2,0,1:T(2,128)(2,1)S(1)} fusion(bf16[2,6,4096]{2,0,1:T(2,128)(2,1)} %param.13, bf16[2,18,4096]{2,0,1:T(2,128)(2,1)} %param.10), kind=kLoop, calls=%fused_computation.2 | loop fusion | flops 196608 | bytes 786432 | tf_op jit(solution)/shard_map/concatenate | solution.py:241
  6.0 0.5 reshape.606
  6.5 0.8 copy.24
  7.3 1.1 reshape.607.own
  8.4 127.1 %ladder_ring.1 = f32[4,512,128]{2,1,0:T(8,128)} custom-call(bf16[2,2,12,32,128]{4,3,2,1,0:T(8,128)(2,1)} %reshape.607.own, s32[2,1,128]{2,1,0:T(1,128)} %bitcast.15, s32[64]{0:T(128)} %reshape.609.loc, bf16[1536,512]{1,0:T(8,128)(2,1)} %lad.1, bf16[512,512]{1,0:T(8,128)(2,1)} %cyc.1), custom_call_target="tpu_custom_call" | custom-call | tf_op jit(solution)/shard_map/ladder_ring/pallas_call | solution.py:269
  135.5 0.0 copy-start
  135.5 1.6 %copy.20 = f32[512,4,128]{0,2,1:T(8,128)S(1)} copy(f32[512,4,128]{2,0,1:T(8,128)} %bitcast.12) | data formatting | bytes 2097152 | tf_op jit(solution)/shard_map/transpose | solution.py:294
  137.2 0.0 copy-done
  137.2 0.3 copy.21
  137.5 0.2 bitcast_add_fusion
  137.8 1.3 copy.22
  (5 shorter events, 0.0 us)
Async XLA Ops:
  135.5 1.7 %copy-start = (f32[512,512]{1,0:T(8,128)S(1)}, f32[512,512]{1,0:T(8,128)}, u32[]{:S(2)}) copy-start(f32[512,512]{1,0:T(8,128)} %param.19) | copy-start | bytes 3145732

commit v2 on v1

v2 whole, which is shorter than its diff:
```python
import jax
import jax.numpy as jnp
from jax import lax
from jax.experimental import pallas as pl
from jax.experimental.pallas import tpu as pltpu
from jax.sharding import PartitionSpec as P

TS = 64
KLT = 24
KRT = 8
MESH = pl.DeviceIdType.MESH
STEPS = 16
PAIRS = 12
HALF = 32
KCAP_L = 18
KCAP_R = 6
CUTS = 2
CUT = PAIRS // CUTS
ZERO = PAIRS
VAR = PAIRS + 1


def pos_first(z, y):
    return 4 * z + (y + z) % 4


def dev_first(s):
    k = s // 4
    return 4 * k + (s % 4 + 32 - k) % 4


def pos_second(z, y):
    t = (z + 24 - 3 * y) % 8
    return 4 * y + 16 * (t // 4) + t % 4


def dev_second(s):
    k = s // 4
    return 4 * ((3 * k + s % 4) % 8) + k % 4


POS = (pos_first, pos_second)
DEV = (dev_first, dev_second)


def kernel(
    own, lad_ids, lad_n, cyc_ids, cyc_n, owners, lad, cyc, out,
    held, tab_own, tab_v, tab_s, loc, panel, spread, lhs, part, got, total, fin_s, fin_r,
    local_sem, pair_s, pair_r, tab_ss, tab_rs, tab_ls, ring_s, ring_r,
    red_s, red_r, sh_s, sh_r, fin_ss, fin_rs,
):
    g = lax.axis_index("grp")
    d = lax.axis_index("dev")
    x = g // 2
    c = g % 2
    z = d // 4
    y = d % 4
    other = 1 - c
    mate = (2 * x + other, d)
    pos = [POS[h](z, y) for h in range(2)]
    nxt = [(g, DEV[h]((pos[h] + 1) % 32)) for h in range(2)]
    prv = [(g, DEV[h]((pos[h] + 31) % 32)) for h in range(2)]

    def local(i, src, dst):
        return pltpu.make_async_copy(src, dst, local_sem.at[i])

    def to_mate(i, src, dst):
        return pltpu.make_async_remote_copy(
            src_ref=src, dst_ref=dst, send_sem=pair_s.at[i], recv_sem=pair_r.at[i],
            device_id=mate, device_id_type=MESH)

    own_here = [local(h, own.at[c, h], held.at[h, 0, c]) for h in range(2)]
    panels_here = [
        local(2, lad, panel.at[c, pl.ds(0, 1536)]),
        local(3, cyc, panel.at[c, pl.ds(1536, 512)]),
    ]
    for copy in own_here + panels_here:
        copy.start()

    barrier = pltpu.get_barrier_semaphore()
    peers = nxt + prv + [mate] + [(2 * ((x + r) % 4) + c, d) for r in (1, 2, 3)]
    for p in peers:
        pl.semaphore_signal(barrier, inc=1, device_id=p, device_id_type=MESH)

    lane = lax.broadcasted_iota(jnp.int32, (1, 128), 1)
    for t in range(2):
        row = jnp.full((1, 128), ZERO, jnp.int32)
        for slot in range(KCAP_L + KCAP_R):
            if slot < KCAP_L:
                tile, live = lad_ids[t, slot], slot < lad_n[t, 0]
            else:
                tile, live = cyc_ids[t, slot - KCAP_L] + KLT, slot - KCAP_L < cyc_n[t, 0]
            code = VAR * ((slot % 2 + tile) % 2) + slot // 2
            row = jnp.where(lane == jnp.where(live, tile, -1), code, row)
        tab_own[t] = row
    for h in range(2):
        tab_v[h, 0, c] = tab_own[c]

    pl.semaphore_wait(barrier, len(peers))

    def mates(side):
        return [
            to_mate(0, own.at[other, 0], held.at[0, 0, side]),
            to_mate(1, own.at[other, 1], held.at[1, 0, side]),
            to_mate(2, tab_own.at[other], tab_v.at[0, 0, side]),
            to_mate(3, tab_own.at[other], tab_v.at[1, 0, side]),
            to_mate(4, lad, panel.at[side, pl.ds(0, 1536)]),
            to_mate(5, cyc, panel.at[side, pl.ds(1536, 512)]),
        ]

    going = mates(c)
    coming = mates(other)
    for copy in going:
        copy.start()

    def hop(h, up, src, dst, kg, piece):
        rows = pl.ds(CUT * piece, CUT)
        return pltpu.make_async_remote_copy(
            src_ref=held.at[h, src, kg, rows], dst_ref=held.at[h, dst, kg, rows],
            send_sem=ring_s.at[h, dst, kg, piece], recv_sem=ring_r.at[h, dst, kg, piece],
            device_id=nxt[h] if up else prv[h], device_id_type=MESH)

    def tab_hop(h, up, src, dst):
        return pltpu.make_async_remote_copy(
            src_ref=tab_v.at[h, src], dst_ref=tab_v.at[h, dst],
            send_sem=tab_ss.at[h, dst], recv_sem=tab_rs.at[h, dst],
            device_id=nxt[h] if up else prv[h], device_id_type=MESH)

    def tab_down(h, slot):
        return pltpu.make_async_copy(tab_v.at[h, slot], tab_s.at[h, slot], tab_ls.at[h, slot])

    for copy in own_here:
        copy.wait()
    for piece in range(CUTS):
        for h in range(2):
            hop(h, True, 0, 1, c, piece).start()
            hop(h, False, 0, 31, c, piece).start()
    for h in range(2):
        coming[2 + h].wait_recv()
        tab_hop(h, True, 0, 1).start()
        tab_hop(h, False, 0, 31).start()
        tab_down(h, 0).start()
    for h in range(2):
        coming[h].wait_recv()
        for piece in range(CUTS):
            hop(h, True, 0, 1, other, piece).start()
            hop(h, False, 0, 31, other, piece).start()

    spread[ZERO] = jnp.zeros((HALF, 128), jnp.bfloat16)
    spread[VAR + ZERO] = jnp.zeros((HALF, 128), jnp.bfloat16)

    @pl.loop(0, 32)
    def _(i):
        tile = owners[16 * (i // 8) + 8 * c + i % 8]
        src = tile // 2
        for h in range(2):
            m = (pos[h] + 32 - POS[h](src // 4, src % 4)) % 32
            far = jnp.where(m >= STEPS, 1, 0)
            b = jnp.where(m >= STEPS, 31 - m, m)
            loc[2 * i + h] = (tile % 2 * STEPS + b) * 4 + 2 * h + far

    left = lax.broadcasted_iota(jnp.int32, (HALF, 128), 1) < 64

    def reduce_copy(b, r):
        to = (x + r) % 4
        return pltpu.make_async_remote_copy(
            src_ref=part.at[b, to], dst_ref=got.at[b, r - 1],
            send_sem=red_s.at[b, r - 1], recv_sem=red_r.at[b, r - 1],
            device_id=(2 * to + c, d), device_id_type=MESH)

    def share_copy(b, side):
        rows = total.at[pl.ds((side * STEPS + b) * 4, 4)]
        return pltpu.make_async_remote_copy(
            src_ref=rows, dst_ref=rows, send_sem=sh_s.at[b], recv_sem=sh_r.at[b],
            device_id=mate, device_id_type=MESH)

    def finish(b):
        for r in (1, 2, 3):
            reduce_copy(b, r).wait_recv()
        s = part[b, x] + got[b, 0] + got[b, 1] + got[b, 2]
        for q in range(4):
            total[(c * STEPS + b) * 4 + q] = s[HALF * q:HALF * (q + 1)]
        share_copy(b, c).start()

    def compute(b):
        for h in range(2):
            tab_down(h, b).wait()
            tab_down(h, 31 - b).wait()
        for kg in range(2):
            for q in range(4):
                h = q // 2
                m = b if q % 2 == 0 else 31 - b
                for p in range(PAIRS):
                    v = held[h, m, kg, p]
                    spread[p] = v
                    spread[VAR + p] = jnp.concatenate([v[:, 64:], v[:, :64]], axis=1)
                for j in range(16):
                    a = tab_s[h, m, kg, 0, 2 * j]
                    e = tab_s[h, m, kg, 0, 2 * j + 1]
                    lhs[HALF * q:HALF * (q + 1), 128 * j:128 * (j + 1)] = jnp.where(left, spread[a], spread[e])
            prod = jnp.dot(lhs[...], panel[kg], preferred_element_type=jnp.float32)
            for q in range(4):
                piece = prod[:, 128 * q:128 * (q + 1)]
                part[b, q] = piece if kg == 0 else part[b, q] + piece
        for r in (2, 1, 3):
            reduce_copy(b, r).start()

    @pl.loop(0, STEPS)
    def _(b):
        for h in range(2):
            @pl.when(b < 15)
            def _():
                tab_hop(h, True, b, b + 1).wait_recv()
                tab_down(h, b + 1).start()

            @pl.when(b < 14)
            def _():
                tab_hop(h, True, b + 1, b + 2).start()

            tab_hop(h, False, 0, 31 - b).wait_recv()
            tab_down(h, 31 - b).start()

            @pl.when(b < 15)
            def _():
                tab_hop(h, False, 31 - b, 30 - b).start()

        for kg in range(2):
            for piece in range(CUTS):
                up_end, down_end = (15, 14) if kg == 0 else (14, 15)
                for h in range(2):
                    @pl.when(b < 15)
                    def _():
                        hop(h, True, b, b + 1, kg, piece).wait_recv()

                    @pl.when(b < up_end)
                    def _():
                        hop(h, True, b + 1, b + 2, kg, piece).start()

                    hop(h, False, 0, 31 - b, kg, piece).wait_recv()

                    @pl.when(b < down_end)
                    def _():
                        hop(h, False, 31 - b, 30 - b, kg, piece).start()

        @pl.when(b == 2)
        def _():
            for copy in panels_here:
                copy.wait()
            for copy in coming[4:]:
                copy.wait_recv()

        first = jnp.where(b < 3, 0, jnp.where(b < 4, 2, b))
        last = jnp.where(b < 2, 0, jnp.where(b < 3, 2, b + 1))

        @pl.loop(first, last)
        def _(i):
            compute(i)

            @pl.when(i >= 2)
            def _():
                finish(i - 2)

    finish(STEPS - 2)
    finish(STEPS - 1)

    @pl.loop(0, STEPS)
    def _(b):
        share_copy(b, other).wait_recv()

    def final_copy(r):
        to = (x + r) % 4
        return pltpu.make_async_remote_copy(
            src_ref=fin_s.at[r], dst_ref=fin_r.at[r - 1], send_sem=fin_ss.at[r - 1], recv_sem=fin_rs.at[r - 1],
            device_id=(2 * to + c, d), device_id_type=MESH)

    for r in (2, 1, 3, 0):
        to = (x + r) % 4
        for i in range(16):
            fin_s[r, HALF * i:HALF * (i + 1)] = total[loc[to * 16 + i]]
        if r:
            final_copy(r).start()
    def columns(of):
        return pl.ds(pl.multiple_of(128 * of, 128), 128)

    out[:, columns(x)] = fin_s[0]
    for r in (1, 3, 2):
        final_copy(r).wait_recv()
        out[:, columns((x + 4 - r) % 4)] = fin_r[r - 1]

    for copy in going:
        copy.wait_send()
    for r in (1, 2, 3):
        final_copy(r).wait_send()

    @pl.loop(0, STEPS)
    def _(b):
        share_copy(b, c).wait_send()
        for r in (1, 2, 3):
            reduce_copy(b, r).wait_send()

    @pl.loop(1, 32)
    def _(m):
        for h in range(2):
            tab_hop(h, True, 0, m).wait_send()
            for kg in range(2):
                for piece in range(CUTS):
                    hop(h, True, 0, m, kg, piece).wait_send()


def per_device(
    ladder_amps, ladder_ids, ladder_count, cycle_amps, cycle_ids, cycle_count,
    ladder_panel, cycle_panel, owners, base,
):
    i32 = jnp.int32
    amps = jnp.concatenate([ladder_amps, cycle_amps], axis=1)
    own = amps.reshape(2, PAIRS, 2, 2, HALF, TS).transpose(0, 3, 1, 4, 2, 5).reshape(2, 2, PAIRS, HALF, 128)

    hbm = pl.BlockSpec(memory_space=pl.ANY)
    smem = pl.BlockSpec(memory_space=pltpu.SMEM)
    bf16, f32 = jnp.bfloat16, jnp.float32
    dma = pltpu.SemaphoreType.DMA
    summed = pl.pallas_call(
        kernel,
        name="ladder_ring",
        out_shape=jax.ShapeDtypeStruct((512, 512), f32),
        in_specs=[hbm] + [smem] * 5 + [hbm, hbm],
        out_specs=pl.BlockSpec(memory_space=pltpu.VMEM),
        scratch_shapes=[
            pltpu.VMEM((2, 32, 2, PAIRS, HALF, 128), bf16),
            pltpu.VMEM((2, 1, 128), i32),
            pltpu.VMEM((2, 32, 2, 1, 128), i32),
            pltpu.SMEM((2, 32, 2, 1, 128), i32),
            pltpu.SMEM((64,), i32),
            pltpu.VMEM((2, 2048, 512), bf16),
            pltpu.VMEM((2 * VAR, HALF, 128), bf16),
            pltpu.VMEM((128, 2048), bf16),
            pltpu.VMEM((STEPS, 4, 128, 128), f32),
            pltpu.VMEM((STEPS, 3, 128, 128), f32),
            pltpu.VMEM((2 * STEPS * 4, HALF, 128), f32),
            pltpu.VMEM((4, 512, 128), f32),
            pltpu.VMEM((3, 512, 128), f32),
            dma((4,)), dma((6,)), dma((6,)), dma((2, 32)), dma((2, 32)), dma((2, 32)),
            dma((2, 32, 2, CUTS)), dma((2, 32, 2, CUTS)),
            dma((STEPS, 3)), dma((STEPS, 3)), dma((STEPS,)), dma((STEPS,)),
            dma((3,)), dma((3,)),
        ],
        compiler_params=pltpu.CompilerParams(has_side_effects=True, collective_id=0, vmem_limit_bytes=58 * 2**20),
    )(own, ladder_ids, ladder_count, cycle_ids, cycle_count, owners, ladder_panel, cycle_panel)
    return base + summed


def solution(mesh):
    placed = (
        P("dev", "grp", None),
        P("dev", "grp"),
        P("dev", "grp"),
        P("dev", "grp", None),
        P("dev", "grp"),
        P("dev", "grp"),
        P("grp", "dev"),
        P("grp", "dev"),
        P(),
        P("grp", "dev"),
    )
    return jax.shard_map(
        per_device, mesh=mesh, in_specs=placed, out_specs=P("grp", "dev"), check_vma=False
    )
```

time: 139 us -> 123 us (0.88)
  Pallas kernels: 127 us -> 115 us
  local copies, waits for them, and re-layouts: 7.22 us -> 3.74 us
    pallas_call x1, Pallas kernels: 127 us -> 115 us  [per_device(): pl.pallas_call(kernel, name='ladder_ring', out_shape=jax.ShapeDtypeStruct...]
    transpose x1 -> x0, local copies, waits for them, and re-layouts: 1.64 us -> none  [per_device(): return base + summed.transpose(1, 0, 2).reshape(512, 512)]
    reshape x2 -> x0, local copies, waits for them, and re-layouts: 1.42 us -> none  [the longest x1 0.74 us: per_device(): tiles = owners.reshape(4, 2, 8)[:, c]]
where the time goes in v2:
time: 123 us; the launch traced here: 122 us
  Pallas kernels  115 us (93%)
  other arithmetic  3.93 us (3%)
  local copies, waits for them, and re-layouts  3.74 us (3%)
    pallas_call x1, Pallas kernels, per_device(): pl.pallas_call(kernel, name='ladder_ring', out_shape=jax.ShapeDtypeStruct...  115 us

profile of v2, /device:TPU:1, one launch (start us, length us, event | category | flops | bytes accessed | tf_op | source)
XLA Modules:
  0.0 122.4 jit_solution(15978263592838880754)
XLA Ops:
  0.0 1.5 %pad_maximum_fusion = bf16[2,24,4096]{2,0,1:T(2,128)(2,1)S(1)} fusion(bf16[2,6,4096]{2,0,1:T(2,128)(2,1)} %param.13, bf16[2,18,4096]{2,0,1:T(2,128)(2,1)} %param.10), kind=kLoop, calls=%fused_computation.1 | loop fusion | flops 196608 | bytes 786432 | tf_op jit(solution)/shard_map/concatenate | solution.py:315
  1.5 0.5 reshape.6
  2.0 0.0 copy-start.1
  2.0 0.0 copy-start.2
  2.1 0.8 copy.15
  2.9 1.1 reshape.7.own
  4.0 0.0 copy-done.1
  4.0 0.7 copy.12.lad_n
  4.6 0.0 copy-done.2
  4.6 0.7 copy.13.cyc_n
  5.3 0.0 copy-start
  5.3 114.7 %ladder_ring.1 = f32[512,512]{1,0:T(8,128)} custom-call(bf16[2,2,12,32,128]{4,3,2,1,0:T(8,128)(2,1)} %reshape.7.own, s32[2,18]{1,0:T(2,128)} %lad_ids.1, s32[2,1]{1,0:T(2,128)} %copy.12.lad_n, s32[2,6]{1,0:T(2,128)} %cyc_ids.1, s32[2,1]{1,0:T(2,128)} %copy.13.cyc_n, s32[64]{0:T(128)} %owners.1, bf16[1536,512]{1,0:T(8,128)(2,1)} %lad.1, bf16[512,512]{1,0:T(8,128)(2,1)} %cyc.1), custom_call_target="tpu_custom_call" | custom-call | tf_op jit(solution)/shard_map/ladder_ring/pallas_call | solution.py:322
  120.0 0.0 copy-done
  120.0 2.4 %add.3 = f32[512,512]{1,0:T(8,128)} add(f32[512,512]{1,0:T(8,128)S(1)} %copy-done, f32[512,512]{1,0:T(8,128)} %ladder_ring.1) | non-fusion elementwise | flops 262144 | bytes 3145728 | tf_op jit(solution)/shard_map/add | solution.py:349
Async XLA Ops:
  2.0 1.9 %copy-start.1 = (s32[2,1]{0,1:T(1,128)S(1)}, s32[2,1]{0,1:T(1,128)}, u32[]{:S(2)}) copy-start(s32[2,1]{0,1:T(1,128)} %param.12) | copy-start | bytes 28
  2.0 2.6 %copy-start.2 = (s32[2,1]{0,1:T(1,128)S(1)}, s32[2,1]{0,1:T(1,128)}, u32[]{:S(2)}) copy-start(s32[2,1]{0,1:T(1,128)} %param.15) | copy-start | bytes 28
  5.3 114.7 %copy-start = (f32[512,512]{1,0:T(8,128)S(1)}, f32[512,512]{1,0:T(8,128)}, u32[]{:S(2)}) copy-start(f32[512,512]{1,0:T(8,128)} %param.19) | copy-start | bytes 3145732

commit v3 on v2

v3 whole, which is shorter than its diff:
```python
import jax
import jax.numpy as jnp
from jax import lax
from jax.experimental import pallas as pl
from jax.experimental.pallas import tpu as pltpu
from jax.sharding import PartitionSpec as P

TS = 64
KLT = 24
KRT = 8
MESH = pl.DeviceIdType.MESH
STEPS = 16
HALF = 32
KCAP_L = 18
KCAP_R = 6
SLOTS = KCAP_L + KCAP_R
CUTS = 2
CUT = SLOTS // CUTS
ZERO = SLOTS
VAR = SLOTS + 1


def pos_first(z, y):
    return 4 * z + (y + z) % 4


def dev_first(s):
    k = s // 4
    return 4 * k + (s % 4 + 32 - k) % 4


def pos_second(z, y):
    t = (z + 24 - 3 * y) % 8
    return 4 * y + 16 * (t // 4) + t % 4


def dev_second(s):
    k = s // 4
    return 4 * ((3 * k + s % 4) % 8) + k % 4


POS = (pos_first, pos_second)
DEV = (dev_first, dev_second)


def kernel(
    lad_own, cyc_own, lad_ids, lad_n, cyc_ids, cyc_n, owners, lad, cyc, out,
    held, tab_own, tab_v, tab_s, loc, panel, spread, lhs, part, got, total, fin_s, fin_r,
    local_sem, pair_s, pair_r, tab_ss, tab_rs, tab_ls, ring_s, ring_r,
    red_s, red_r, sh_s, sh_r, fin_ss, fin_rs,
):
    g = lax.axis_index("grp")
    d = lax.axis_index("dev")
    x = g // 2
    c = g % 2
    z = d // 4
    y = d % 4
    other = 1 - c
    mate = (2 * x + other, d)
    across = [(x + r) % 4 for r in range(4)]
    pos = [POS[h](z, y) for h in range(2)]
    nxt = [(g, DEV[h]((pos[h] + 1) % 32)) for h in range(2)]
    prv = [(g, DEV[h]((pos[h] + 31) % 32)) for h in range(2)]

    def local(i, src, dst):
        return pltpu.make_async_copy(src, dst, local_sem.at[i])

    def to_mate(i, src, dst):
        return pltpu.make_async_remote_copy(
            src_ref=src, dst_ref=dst, send_sem=pair_s.at[i], recv_sem=pair_r.at[i],
            device_id=mate, device_id_type=MESH)

    def own_parts(h, tile, side):
        return [
            (lad_own.at[:, tile, h], held.at[h, 0, side, pl.ds(0, KCAP_L)]),
            (cyc_own.at[:, tile, h], held.at[h, 0, side, pl.ds(KCAP_L, KCAP_R)]),
        ]

    own_here = [local(2 * h + i, *own_parts(h, c, c)[i]) for h in range(2) for i in range(2)]
    panels_here = [
        local(4, lad, panel.at[c, pl.ds(0, 1536)]),
        local(5, cyc, panel.at[c, pl.ds(1536, 512)]),
    ]
    for copy in own_here + panels_here:
        copy.start()

    barrier = pltpu.get_barrier_semaphore()
    peers = nxt + prv + [mate] + [(2 * across[r] + c, d) for r in (1, 2, 3)]
    for p in peers:
        pl.semaphore_signal(barrier, inc=1, device_id=p, device_id_type=MESH)

    lane = lax.broadcasted_iota(jnp.int32, (1, 128), 1)
    for t in range(2):
        row = jnp.full((1, 128), ZERO, jnp.int32)
        for slot in range(KCAP_L + KCAP_R):
            if slot < KCAP_L:
                tile, live = lad_ids[t, slot], slot < lad_n[t]
            else:
                tile, live = cyc_ids[t, slot - KCAP_L] + KLT, slot - KCAP_L < cyc_n[t]
            row = jnp.where(lane == jnp.where(live, tile, -1), slot, row)
        tab_own[t] = row
    for h in range(2):
        tab_v[h, 0, c] = tab_own[c]

    pl.semaphore_wait(barrier, len(peers))

    def mates(side):
        return [
            to_mate(2 * h + i, *own_parts(h, other, side)[i]) for h in range(2) for i in range(2)
        ] + [
            to_mate(4, tab_own.at[other], tab_v.at[0, 0, side]),
            to_mate(5, tab_own.at[other], tab_v.at[1, 0, side]),
            to_mate(6, lad, panel.at[side, pl.ds(0, 1536)]),
            to_mate(7, cyc, panel.at[side, pl.ds(1536, 512)]),
        ]

    going = mates(c)
    coming = mates(other)
    for copy in going:
        copy.start()

    def hop(h, up, src, dst, kg, piece):
        rows = pl.ds(CUT * piece, CUT)
        return pltpu.make_async_remote_copy(
            src_ref=held.at[h, src, kg, rows], dst_ref=held.at[h, dst, kg, rows],
            send_sem=ring_s.at[h], recv_sem=ring_r.at[h, dst, kg, piece],
            device_id=nxt[h] if up else prv[h], device_id_type=MESH)

    def tab_hop(h, up, src, dst):
        return pltpu.make_async_remote_copy(
            src_ref=tab_v.at[h, src], dst_ref=tab_v.at[h, dst],
            send_sem=tab_ss.at[h], recv_sem=tab_rs.at[h, dst],
            device_id=nxt[h] if up else prv[h], device_id_type=MESH)

    def tab_down(h, slot):
        return pltpu.make_async_copy(tab_v.at[h, slot], tab_s.at[h, slot], tab_ls.at[h, slot])

    for copy in own_here:
        copy.wait()
    for piece in range(CUTS):
        for h in range(2):
            hop(h, True, 0, 1, c, piece).start()
            hop(h, False, 0, 31, c, piece).start()
    for h in range(2):
        coming[4 + h].wait_recv()
        tab_hop(h, True, 0, 1).start()
        tab_hop(h, False, 0, 31).start()
        tab_down(h, 0).start()
    for h in range(2):
        coming[2 * h].wait_recv()
        coming[2 * h + 1].wait_recv()
        for piece in range(CUTS):
            hop(h, True, 0, 1, other, piece).start()
            hop(h, False, 0, 31, other, piece).start()

    spread[ZERO] = jnp.zeros((16, 128), jnp.bfloat16)
    spread[VAR + ZERO] = jnp.zeros((16, 128), jnp.bfloat16)

    def seat(h, row, col):
        if h == 0:
            return 4 * row + ((col + row) & 3)
        t = (row + 24 - 3 * col) & 7
        return 4 * col + 16 * (t >> 2) + (t & 3)

    @pl.loop(0, 4)
    def _(to):
        for i in range(8):
            tile = owners[16 * to + 8 * c + i]
            row, col = tile >> 3, (tile >> 1) & 3
            for h in range(2):
                m = (pos[h] + 32 - seat(h, row, col)) & 31
                near = m < STEPS
                b = jnp.where(near, m, 31 - m)
                q = jnp.where(near, 2 * h, 2 * h + 1)
                loc[16 * to + 2 * i + h] = 4 * (STEPS * (tile & 1) + b) + q

    left = lax.broadcasted_iota(jnp.int32, (16, 128), 1) < 64

    def reduce_copy(b, r):
        to = across[r]
        return pltpu.make_async_remote_copy(
            src_ref=part.at[b, to], dst_ref=got.at[b, r - 1],
            send_sem=red_s, recv_sem=red_r.at[b, r - 1],
            device_id=(2 * to + c, d), device_id_type=MESH)

    def share_copy(b, side):
        rows = total.at[pl.ds((side * STEPS + b) * 4, 4)]
        return pltpu.make_async_remote_copy(
            src_ref=rows, dst_ref=rows, send_sem=sh_s, recv_sem=sh_r.at[b],
            device_id=mate, device_id_type=MESH)

    def finish(b):
        for r in (1, 2, 3):
            reduce_copy(b, r).wait_recv()
        s = part[b, x] + got[b, 0] + got[b, 1] + got[b, 2]
        for q in range(4):
            total[(c * STEPS + b) * 4 + q] = s[HALF * q:HALF * (q + 1)]
        share_copy(b, c).start()

    def compute(b):
        for h in range(2):
            tab_down(h, b).wait()
            tab_down(h, 31 - b).wait()
        for kg in range(2):
            for q in range(4):
                h = q // 2
                m = b if q % 2 == 0 else 31 - b
                for p in range(SLOTS):
                    v = held[h, m, kg, p]
                    spread[p] = v
                    spread[VAR + p] = jnp.concatenate([v[:, 64:], v[:, :64]], axis=1)
                for j in range(16):
                    a = tab_s[h, m, kg, 0, 2 * j]
                    e = tab_s[h, m, kg, 0, 2 * j + 1]
                    at = slice(128 * j, 128 * (j + 1))
                    lhs[HALF * q:HALF * q + 16, at] = jnp.where(left, spread[a], spread[VAR + e])
                    lhs[HALF * q + 16:HALF * (q + 1), at] = jnp.where(left, spread[VAR + a], spread[e])
            prod = jnp.dot(lhs[...], panel[kg], preferred_element_type=jnp.float32)
            for q in range(4):
                piece = prod[:, 128 * q:128 * (q + 1)]
                part[b, q] = piece if kg == 0 else part[b, q] + piece
        for r in (2, 1, 3):
            reduce_copy(b, r).start()

    @pl.loop(0, STEPS)
    def _(b):
        for h in range(2):
            @pl.when(b < 15)
            def _():
                tab_hop(h, True, b, b + 1).wait_recv()
                tab_down(h, b + 1).start()

            @pl.when(b < 14)
            def _():
                tab_hop(h, True, b + 1, b + 2).start()

            tab_hop(h, False, 0, 31 - b).wait_recv()
            tab_down(h, 31 - b).start()

            @pl.when(b < 15)
            def _():
                tab_hop(h, False, 31 - b, 30 - b).start()

        for kg in range(2):
            for piece in range(CUTS):
                up_end, down_end = (15, 14) if kg == 0 else (14, 15)
                for h in range(2):
                    @pl.when(b < 15)
                    def _():
                        hop(h, True, b, b + 1, kg, piece).wait_recv()

                    @pl.when(b < up_end)
                    def _():
                        hop(h, True, b + 1, b + 2, kg, piece).start()

                    hop(h, False, 0, 31 - b, kg, piece).wait_recv()

                    @pl.when(b < down_end)
                    def _():
                        hop(h, False, 31 - b, 30 - b, kg, piece).start()

        @pl.when(b == 2)
        def _():
            for copy in panels_here:
                copy.wait()
            for copy in coming[6:]:
                copy.wait_recv()

        first = jnp.where(b < 3, 0, jnp.where(b < 4, 2, b))
        last = jnp.where(b < 2, 0, jnp.where(b < 3, 2, b + 1))

        @pl.loop(first, last)
        def _(i):
            compute(i)

            @pl.when(i >= 2)
            def _():
                finish(i - 2)

    finish(STEPS - 2)
    finish(STEPS - 1)

    @pl.loop(0, STEPS)
    def _(b):
        share_copy(b, other).wait_recv()

    def final_copy(r):
        to = across[r]
        return pltpu.make_async_remote_copy(
            src_ref=fin_s.at[r], dst_ref=fin_r.at[r - 1], send_sem=fin_ss, recv_sem=fin_rs.at[r - 1],
            device_id=(2 * to + c, d), device_id_type=MESH)

    for r in (2, 1, 3, 0):
        to = across[r]
        for i in range(16):
            rows = total[loc[to * 16 + i]]
            fin_s[r, pl.ds(HALF * i, 16, stride=2)] = rows[:16]
            fin_s[r, pl.ds(HALF * i + 1, 16, stride=2)] = rows[16:]
        if r:
            final_copy(r).start()
    def columns(of):
        return pl.ds(pl.multiple_of(128 * of, 128), 128)

    out[:, columns(x)] = fin_s[0]

    def drain(ref, sem):
        pltpu.make_async_copy(ref, ref, sem).wait()

    for copy in going:
        copy.wait_send()
    for h in range(2):
        drain(held.at[h, pl.ds(0, 31)], ring_s.at[h])
        drain(tab_v.at[h, pl.ds(0, 31)], tab_ss.at[h])
    drain(got, red_s)
    drain(total.at[pl.ds(0, 4 * STEPS)], sh_s)

    for r in (1, 3, 2):
        final_copy(r).wait_recv()
        out[:, columns(across[4 - r])] = fin_r[r - 1]
    drain(fin_r, fin_ss)


def per_device(
    ladder_amps, ladder_ids, ladder_count, cycle_amps, cycle_ids, cycle_count,
    ladder_panel, cycle_panel, owners, base,
):
    i32 = jnp.int32
    lad_own = ladder_amps.transpose(1, 0, 2).reshape(KCAP_L, 2, 2, 16, 128)
    cyc_own = cycle_amps.transpose(1, 0, 2).reshape(KCAP_R, 2, 2, 16, 128)
    lad_n, cyc_n = ladder_count.reshape(2), cycle_count.reshape(2)

    hbm = pl.BlockSpec(memory_space=pl.ANY)
    smem = pl.BlockSpec(memory_space=pltpu.SMEM)
    bf16, f32 = jnp.bfloat16, jnp.float32
    dma = pltpu.SemaphoreType.DMA
    summed = pl.pallas_call(
        kernel,
        name="ladder_ring",
        out_shape=jax.ShapeDtypeStruct((512, 512), f32),
        in_specs=[hbm] * 2 + [smem] * 5 + [hbm, hbm],
        out_specs=pl.BlockSpec(memory_space=pltpu.VMEM),
        scratch_shapes=[
            pltpu.VMEM((2, 32, 2, SLOTS, 16, 128), bf16),
            pltpu.VMEM((2, 1, 128), i32),
            pltpu.VMEM((2, 32, 2, 1, 128), i32),
            pltpu.SMEM((2, 32, 2, 1, 128), i32),
            pltpu.SMEM((64,), i32),
            pltpu.VMEM((2, 2048, 512), bf16),
            pltpu.VMEM((2 * VAR, 16, 128), bf16),
            pltpu.VMEM((128, 2048), bf16),
            pltpu.VMEM((STEPS, 4, 128, 128), f32),
            pltpu.VMEM((STEPS, 3, 128, 128), f32),
            pltpu.VMEM((2 * STEPS * 4, HALF, 128), f32),
            pltpu.VMEM((4, 512, 128), f32),
            pltpu.VMEM((3, 512, 128), f32),
            dma((6,)), dma((8,)), dma((8,)), dma((2,)), dma((2, 32)), dma((2, 32)),
            dma((2,)), dma((2, 32, 2, CUTS)),
            dma, dma((STEPS, 3)), dma, dma((STEPS,)), dma, dma((3,)),
        ],
        compiler_params=pltpu.CompilerParams(has_side_effects=True, collective_id=0, vmem_limit_bytes=58 * 2**20),
    )(lad_own, cyc_own, ladder_ids, lad_n, cycle_ids, cyc_n, owners, ladder_panel, cycle_panel)
    return base + summed


def solution(mesh):
    placed = (
        P("dev", "grp", None),
        P("dev", "grp"),
        P("dev", "grp"),
        P("dev", "grp", None),
        P("dev", "grp"),
        P("dev", "grp"),
        P("grp", "dev"),
        P("grp", "dev"),
        P(),
        P("grp", "dev"),
    )
    return jax.shard_map(
        per_device, mesh=mesh, in_specs=placed, out_specs=P("grp", "dev"), check_vma=False
    )
```

time: 123 us -> 117 us (0.951)
  Pallas kernels: 115 us -> 111 us
  other arithmetic: 3.93 us -> 2.4 us
    pallas_call x1, Pallas kernels: 115 us -> 111 us  [per_device(): pl.pallas_call(kernel, name='ladder_ring', out_shape=jax.ShapeDtypeStruct...]
    concatenate x1 -> x0, other arithmetic: 1.53 us -> none  [per_device(): amps = jnp.concatenate([ladder_amps, cycle_amps], axis=1)]
    unnamed x8 -> x2, local copies, waits for them, and re-layouts: 1.34 us -> 0.01 us
    reshape x3 -> x2, local copies, waits for them, and re-layouts: 2.4 us -> 3.51 us  [the longest x1 1.9 us: per_device(): lad_own = ladder_amps.transpose(1, 0, 2).reshape(KCAP_L, 2, 2, 16, 128)]
where the time goes in v3:
time: 117 us
  Pallas kernels  111 us (95%)
  local copies, waits for them, and re-layouts  3.52 us (3%)
  other arithmetic  2.4 us (2%)
    pallas_call x1, Pallas kernels, per_device(): pl.pallas_call(kernel, name='ladder_ring', out_shape=jax.ShapeDtypeStruct...  111 us
    add x1, other arithmetic, per_device(): return base + summed  2.4 us

profile of v3, /device:TPU:1, one launch (start us, length us, event | category | flops | bytes accessed | tf_op | source)
XLA Modules:
  0.0 116.5 jit_solution(2484756881669453625)
XLA Ops:
  0.0 1.6 %reshape.13.cyc_own = bf16[6,2,2,16,128]{4,3,2,1,0:T(8,128)(2,1)} reshape(bf16[6,2,4096]{2,1,0:T(2,128)(2,1)} %bitcast.5) | data formatting | bytes 196608 | tf_op jit(solution)/shard_map/reshape | solution.py:329
  1.6 1.9 %reshape.12.lad_own = bf16[18,2,2,16,128]{4,3,2,1,0:T(8,128)(2,1)} reshape(bf16[18,2,4096]{2,1,0:T(2,128)(2,1)} %bitcast.4) | data formatting | bytes 589824 | tf_op jit(solution)/shard_map/reshape | solution.py:328
  3.5 0.0 copy-start
  3.5 110.6 %ladder_ring.1 = f32[512,512]{1,0:T(8,128)} custom-call(bf16[18,2,2,16,128]{4,3,2,1,0:T(8,128)(2,1)} %reshape.12.lad_own, bf16[6,2,2,16,128]{4,3,2,1,0:T(8,128)(2,1)} %reshape.13.cyc_own, s32[2,18]{1,0:T(2,128)} %lad_ids.1, s32[2]{0:T(128)} %bitcast.6, s32[2,6]{1,0:T(2,128)} %cyc_ids.1, s32[2]{0:T(128)} %bitcast.7, s32[64]{0:T(128)} %owners.1, ...), custom_call_target="tpu_custom_call" | custom-call | tf_op jit(solution)/shard_map/ladder_ring/pallas_call | solution.py:336
  114.1 0.0 copy-done
  114.1 2.4 %add.3 = f32[512,512]{1,0:T(8,128)} add(f32[512,512]{1,0:T(8,128)S(1)} %copy-done, f32[512,512]{1,0:T(8,128)} %ladder_ring.1) | non-fusion elementwise | flops 262144 | bytes 3145728 | tf_op jit(solution)/shard_map/add | solution.py:362
Async XLA Ops:
  3.5 110.6 %copy-start = (f32[512,512]{1,0:T(8,128)S(1)}, f32[512,512]{1,0:T(8,128)}, u32[]{:S(2)}) copy-start(f32[512,512]{1,0:T(8,128)} %param.19) | copy-start | bytes 3145732

commit v4 on v3

--- a/solution.py
+++ b/solution.py
@@ -44,8 +44,8 @@
 
 
 def kernel(
-    lad_own, cyc_own, lad_ids, lad_n, cyc_ids, cyc_n, owners, lad, cyc, out,
-    held, tab_own, tab_v, tab_s, loc, panel, spread, lhs, part, got, total, fin_s, fin_r,
+    lad_amps, cyc_amps, lad_ids, lad_n, cyc_ids, cyc_n, owners, lad, cyc, base, out,
+    amps_l, amps_c, own, held, tab_own, tab_v, tab_s, loc, panel, spread, lhs, part, got, total, fin_s, fin_r, base_v,
     local_sem, pair_s, pair_r, tab_ss, tab_rs, tab_ls, ring_s, ring_r,
     red_s, red_r, sh_s, sh_r, fin_ss, fin_rs,
 ):
@@ -70,18 +70,13 @@
             src_ref=src, dst_ref=dst, send_sem=pair_s.at[i], recv_sem=pair_r.at[i],
             device_id=mate, device_id_type=MESH)
 
-    def own_parts(h, tile, side):
-        return [
-            (lad_own.at[:, tile, h], held.at[h, 0, side, pl.ds(0, KCAP_L)]),
-            (cyc_own.at[:, tile, h], held.at[h, 0, side, pl.ds(KCAP_L, KCAP_R)]),
-        ]
-
-    own_here = [local(2 * h + i, *own_parts(h, c, c)[i]) for h in range(2) for i in range(2)]
+    amps_here = [local(0, lad_amps, amps_l), local(1, cyc_amps, amps_c)]
     panels_here = [
-        local(4, lad, panel.at[c, pl.ds(0, 1536)]),
-        local(5, cyc, panel.at[c, pl.ds(1536, 512)]),
+        local(2, lad, panel.at[c, pl.ds(0, 1536)]),
+        local(3, cyc, panel.at[c, pl.ds(1536, 512)]),
     ]
-    for copy in own_here + panels_here:
+    base_here = local(4, base, base_v)
+    for copy in amps_here + panels_here + [base_here]:
         copy.start()
 
     barrier = pltpu.get_barrier_semaphore()
@@ -99,19 +94,27 @@
                 tile, live = cyc_ids[t, slot - KCAP_L] + KLT, slot - KCAP_L < cyc_n[t]
             row = jnp.where(lane == jnp.where(live, tile, -1), slot, row)
         tab_own[t] = row
+    for copy in amps_here:
+        copy.wait()
+    for t in range(2):
+        for amps, first, count in ((amps_l, 0, KCAP_L), (amps_c, KCAP_L, KCAP_R)):
+            pairs = amps[:, t, :].reshape(count, HALF, 128)
+            for h in range(2):
+                own[t, h, first:first + count] = pairs[:, 16 * h:16 * (h + 1)]
     for h in range(2):
+        held[h, 0, c] = own[c, h]
         tab_v[h, 0, c] = tab_own[c]
 
     pl.semaphore_wait(barrier, len(peers))
 
     def mates(side):
         return [
-            to_mate(2 * h + i, *own_parts(h, other, side)[i]) for h in range(2) for i in range(2)
-        ] + [
-            to_mate(4, tab_own.at[other], tab_v.at[0, 0, side]),
-            to_mate(5, tab_own.at[other], tab_v.at[1, 0, side]),
-            to_mate(6, lad, panel.at[side, pl.ds(0, 1536)]),
-            to_mate(7, cyc, panel.at[side, pl.ds(1536, 512)]),
+            to_mate(0, own.at[other, 0], held.at[0, 0, side]),
+            to_mate(1, own.at[other, 1], held.at[1, 0, side]),
+            to_mate(2, tab_own.at[other], tab_v.at[0, 0, side]),
+            to_mate(3, tab_own.at[other], tab_v.at[1, 0, side]),
+            to_mate(4, lad, panel.at[side, pl.ds(0, 1536)]),
+            to_mate(5, cyc, panel.at[side, pl.ds(1536, 512)]),
         ]
 
     going = mates(c)
@@ -135,20 +138,17 @@
     def tab_down(h, slot):
         return pltpu.make_async_copy(tab_v.at[h, slot], tab_s.at[h, slot], tab_ls.at[h, slot])
 
-    for copy in own_here:
-        copy.wait()
     for piece in range(CUTS):
         for h in range(2):
             hop(h, True, 0, 1, c, piece).start()
             hop(h, False, 0, 31, c, piece).start()
     for h in range(2):
-        coming[4 + h].wait_recv()
+        coming[2 + h].wait_recv()
         tab_hop(h, True, 0, 1).start()
         tab_hop(h, False, 0, 31).start()
         tab_down(h, 0).start()
     for h in range(2):
-        coming[2 * h].wait_recv()
-        coming[2 * h + 1].wait_recv()
+        coming[h].wait_recv()
         for piece in range(CUTS):
             hop(h, True, 0, 1, other, piece).start()
             hop(h, False, 0, 31, other, piece).start()
@@ -197,30 +197,24 @@
             total[(c * STEPS + b) * 4 + q] = s[HALF * q:HALF * (q + 1)]
         share_copy(b, c).start()
 
-    def compute(b):
-        for h in range(2):
-            tab_down(h, b).wait()
-            tab_down(h, 31 - b).wait()
-        for kg in range(2):
-            for q in range(4):
-                h = q // 2
-                m = b if q % 2 == 0 else 31 - b
-                for p in range(SLOTS):
-                    v = held[h, m, kg, p]
-                    spread[p] = v
-                    spread[VAR + p] = jnp.concatenate([v[:, 64:], v[:, :64]], axis=1)
-                for j in range(16):
-                    a = tab_s[h, m, kg, 0, 2 * j]
-                    e = tab_s[h, m, kg, 0, 2 * j + 1]
-                    at = slice(128 * j, 128 * (j + 1))
-                    lhs[HALF * q:HALF * q + 16, at] = jnp.where(left, spread[a], spread[VAR + e])
-                    lhs[HALF * q + 16:HALF * (q + 1), at] = jnp.where(left, spread[VAR + a], spread[e])
-            prod = jnp.dot(lhs[...], panel[kg], preferred_element_type=jnp.float32)
-            for q in range(4):
-                piece = prod[:, 128 * q:128 * (q + 1)]
-                part[b, q] = piece if kg == 0 else part[b, q] + piece
-        for r in (2, 1, 3):
-            reduce_copy(b, r).start()
+    def compute(b, kg):
+        for q in range(4):
+            h = q // 2
+            m = b if q % 2 == 0 else 31 - b
+            for p in range(SLOTS):
+                v = held[h, m, kg, p]
+                spread[p] = v
+                spread[VAR + p] = jnp.concatenate([v[:, 64:], v[:, :64]], axis=1)
+            for j in range(16):
+                a = tab_s[h, m, kg, 0, 2 * j]
+                e = tab_s[h, m, kg, 0, 2 * j + 1]
+                at = slice(128 * j, 128 * (j + 1))
+                lhs[HALF * q:HALF * q + 16, at] = jnp.where(left, spread[a], spread[VAR + e])
+                lhs[HALF * q + 16:HALF * (q + 1), at] = jnp.where(left, spread[VAR + a], spread[e])
+        prod = jnp.dot(lhs[...], panel[kg], preferred_element_type=jnp.float32)
+        for q in range(4):
+            piece = prod[:, 128 * q:128 * (q + 1)]
+            part[b, q] = piece if kg == 0 else part[b, q] + piece
 
     @pl.loop(0, STEPS)
     def _(b):
@@ -241,6 +235,16 @@
             def _():
                 tab_hop(h, False, 31 - b, 30 - b).start()
 
+        @pl.when(b == 2)
+        def _():
+            for copy in panels_here:
+                copy.wait()
+            for copy in coming[4:]:
+                copy.wait_recv()
+
+        first = jnp.where(b < 3, 0, jnp.where(b < 4, 2, b))
+        last = jnp.where(b < 2, 0, jnp.where(b < 3, 2, b + 1))
+
         for kg in range(2):
             for piece in range(CUTS):
                 up_end, down_end = (15, 14) if kg == 0 else (14, 15)
@@ -259,26 +263,24 @@
                     def _():
                         hop(h, False, 31 - b, 30 - b, kg, piece).start()
 
-        @pl.when(b == 2)
-        def _():
-            for copy in panels_here:
-                copy.wait()
-            for copy in coming[6:]:
-                copy.wait_recv()
-
-        first = jnp.where(b < 3, 0, jnp.where(b < 4, 2, b))
-        last = jnp.where(b < 2, 0, jnp.where(b < 3, 2, b + 1))
-
-        @pl.loop(first, last)
-        def _(i):
-            compute(i)
-
-            @pl.when(i >= 2)
-            def _():
-                finish(i - 2)
-
-    finish(STEPS - 2)
-    finish(STEPS - 1)
+            @pl.loop(first, last)
+            def _(i):
+                if kg == 0:
+                    for h in range(2):
+                        tab_down(h, i).wait()
+                        tab_down(h, 31 - i).wait()
+                compute(i, kg)
+                if kg == 0:
+                    @pl.when(i >= 4)
+                    def _():
+                        finish(i - 4)
+                else:
+                    for r in (2, 1, 3):
+                        reduce_copy(i, r).start()
+
+    @pl.loop(STEPS - 4, STEPS)
+    def _(b):
+        finish(b)
 
     @pl.loop(0, STEPS)
     def _(b):
@@ -301,7 +303,8 @@
     def columns(of):
         return pl.ds(pl.multiple_of(128 * of, 128), 128)
 
-    out[:, columns(x)] = fin_s[0]
+    base_here.wait()
+    out[:, columns(x)] = base_v[:, columns(x)] + fin_s[0]
 
     def drain(ref, sem):
         pltpu.make_async_copy(ref, ref, sem).wait()
@@ -316,7 +319,8 @@
 
     for r in (1, 3, 2):
         final_copy(r).wait_recv()
-        out[:, columns(across[4 - r])] = fin_r[r - 1]
+        cols = columns(across[4 - r])
+        out[:, cols] = base_v[:, cols] + fin_r[r - 1]
     drain(fin_r, fin_ss)
 
 
@@ -325,8 +329,7 @@
     ladder_panel, cycle_panel, owners, base,
 ):
     i32 = jnp.int32
-    lad_own = ladder_amps.transpose(1, 0, 2).reshape(KCAP_L, 2, 2, 16, 128)
-    cyc_own = cycle_amps.transpose(1, 0, 2).reshape(KCAP_R, 2, 2, 16, 128)
+    lad_amps, cyc_amps = ladder_amps.transpose(1, 0, 2), cycle_amps.transpose(1, 0, 2)
     lad_n, cyc_n = ladder_count.reshape(2), cycle_count.reshape(2)
 
     hbm = pl.BlockSpec(memory_space=pl.ANY)
@@ -337,9 +340,12 @@
         kernel,
         name="ladder_ring",
         out_shape=jax.ShapeDtypeStruct((512, 512), f32),
-        in_specs=[hbm] * 2 + [smem] * 5 + [hbm, hbm],
+        in_specs=[hbm] * 2 + [smem] * 5 + [hbm] * 3,
         out_specs=pl.BlockSpec(memory_space=pltpu.VMEM),
         scratch_shapes=[
+            pltpu.VMEM((KCAP_L, 2, TS * TS), bf16),
+            pltpu.VMEM((KCAP_R, 2, TS * TS), bf16),
+            pltpu.VMEM((2, 2, SLOTS, 16, 128), bf16),
             pltpu.VMEM((2, 32, 2, SLOTS, 16, 128), bf16),
             pltpu.VMEM((2, 1, 128), i32),
             pltpu.VMEM((2, 32, 2, 1, 128), i32),
@@ -353,13 +359,14 @@
             pltpu.VMEM((2 * STEPS * 4, HALF, 128), f32),
             pltpu.VMEM((4, 512, 128), f32),
             pltpu.VMEM((3, 512, 128), f32),
-            dma((6,)), dma((8,)), dma((8,)), dma((2,)), dma((2, 32)), dma((2, 32)),
+            pltpu.VMEM((512, 512), f32),
+            dma((5,)), dma((6,)), dma((6,)), dma((2,)), dma((2, 32)), dma((2, 32)),
             dma((2,)), dma((2, 32, 2, CUTS)),
             dma, dma((STEPS, 3)), dma, dma((STEPS,)), dma, dma((3,)),
         ],
         compiler_params=pltpu.CompilerParams(has_side_effects=True, collective_id=0, vmem_limit_bytes=58 * 2**20),
-    )(lad_own, cyc_own, ladder_ids, lad_n, cycle_ids, cyc_n, owners, ladder_panel, cycle_panel)
-    return base + summed
+    )(lad_amps, cyc_amps, ladder_ids, lad_n, cycle_ids, cyc_n, owners, ladder_panel, cycle_panel, base)
+    return summed
 
 
 def solution(mesh):

time: 117 us -> 109 us (0.932)
  Pallas kernels: 111 us -> 107 us
  other arithmetic: 2.4 us -> 0 us
  local copies, waits for them, and re-layouts: 3.52 us -> 2.26 us
    pallas_call x1, Pallas kernels: 111 us -> 107 us  [per_device(): pl.pallas_call(kernel, name='ladder_ring', out_shape=jax.ShapeDtypeStruct...]
    reshape x2 -> x0, local copies, waits for them, and re-layouts: 3.51 us -> none  [the longest x1 1.9 us: per_device(): lad_own = ladder_amps.transpose(1, 0, 2).reshape(KCAP_L, 2, 2, 16, 128)]
    add x1 -> x0, other arithmetic: 2.4 us -> none  [per_device(): return base + summed]
    unnamed x2 -> x1, local copies, waits for them, and re-layouts: 0.01 us -> 2.26 us
where the time goes in v4:
time: 109 us
  Pallas kernels  107 us (98%)
  local copies, waits for them, and re-layouts  2.26 us (2%)
    pallas_call x1, Pallas kernels, per_device(): pl.pallas_call(kernel, name='ladder_ring', out_shape=jax.ShapeDtypeStruct...  107 us
    unnamed x1, local copies, waits for them, and re-layouts  2.26 us

profile of v4, /device:TPU:1, one launch (start us, length us, event | category | flops | bytes accessed | tf_op | source)
XLA Modules:
  0.0 108.9 jit_solution(2630803743040813474)
XLA Ops:
  0.0 106.6 %ladder_ring.1 = f32[512,512]{1,0:T(8,128)} custom-call(bf16[18,2,4096]{2,1,0:T(2,128)(2,1)} %bitcast.4, bf16[6,2,4096]{2,1,0:T(2,128)(2,1)} %bitcast.5, s32[2,18]{1,0:T(2,128)} %lad_ids.1, s32[2]{0:T(128)} %bitcast.6, s32[2,6]{1,0:T(2,128)} %cyc_ids.1, s32[2]{0:T(128)} %bitcast.7, s32[64]{0:T(128)} %owners.1, bf16[1536,512]{1,0:T(8,128)(2,1)} %lad.1, ...), custom_call_target="tpu_custom_call" | custom-call | tf_op jit(solution)/shard_map/ladder_ring/pallas_call | solution.py:339
  106.6 2.3 %copy.12 = f32[512,512]{1,0:T(8,128)} copy(f32[512,512]{1,0:T(8,128)} %ladder_ring.1) | data formatting | bytes 2097152

commit v5 on v4

--- a/solution.py
+++ b/solution.py
@@ -44,7 +44,8 @@
 
 
 def kernel(
-    lad_amps, cyc_amps, lad_ids, lad_n, cyc_ids, cyc_n, owners, lad, cyc, base, out,
+    lad_amps, cyc_amps, lad_ids_h, lad_n_h, cyc_ids_h, cyc_n_h, owners_h, lad, cyc, base, out,
+    lad_ids, lad_n, cyc_ids, cyc_n, owners,
     amps_l, amps_c, own, held, tab_own, tab_v, tab_s, loc, panel, spread, lhs, part, got, total, fin_s, fin_r, base_v,
     local_sem, pair_s, pair_r, tab_ss, tab_rs, tab_ls, ring_s, ring_r,
     red_s, red_r, sh_s, sh_r, fin_ss, fin_rs,
@@ -70,19 +71,25 @@
             src_ref=src, dst_ref=dst, send_sem=pair_s.at[i], recv_sem=pair_r.at[i],
             device_id=mate, device_id_type=MESH)
 
+    barrier = pltpu.get_barrier_semaphore()
+    peers = nxt + prv + [mate] + [(2 * across[r] + c, d) for r in (1, 2, 3)]
+    for p in peers:
+        pl.semaphore_signal(barrier, inc=1, device_id=p, device_id_type=MESH)
+
     amps_here = [local(0, lad_amps, amps_l), local(1, cyc_amps, amps_c)]
     panels_here = [
         local(2, lad, panel.at[c, pl.ds(0, 1536)]),
         local(3, cyc, panel.at[c, pl.ds(1536, 512)]),
     ]
     base_here = local(4, base, base_v)
-    for copy in amps_here + panels_here + [base_here]:
+    lists_here = [
+        local(5, lad_ids_h, lad_ids), local(6, lad_n_h, lad_n),
+        local(7, cyc_ids_h, cyc_ids), local(8, cyc_n_h, cyc_n), local(9, owners_h, owners),
+    ]
+    for copy in amps_here + lists_here + panels_here + [base_here]:
         copy.start()
-
-    barrier = pltpu.get_barrier_semaphore()
-    peers = nxt + prv + [mate] + [(2 * across[r] + c, d) for r in (1, 2, 3)]
-    for p in peers:
-        pl.semaphore_signal(barrier, inc=1, device_id=p, device_id_type=MESH)
+    for copy in lists_here:
+        copy.wait()
 
     lane = lax.broadcasted_iota(jnp.int32, (1, 128), 1)
     for t in range(2):
@@ -171,7 +178,7 @@
                 m = (pos[h] + 32 - seat(h, row, col)) & 31
                 near = m < STEPS
                 b = jnp.where(near, m, 31 - m)
-                q = jnp.where(near, 2 * h, 2 * h + 1)
+                q = jnp.where(near, h, 2 + h)
                 loc[16 * to + 2 * i + h] = 4 * (STEPS * (tile & 1) + b) + q
 
     left = lax.broadcasted_iota(jnp.int32, (16, 128), 1) < 64
@@ -180,6 +187,14 @@
         to = across[r]
         return pltpu.make_async_remote_copy(
             src_ref=part.at[b, to], dst_ref=got.at[b, r - 1],
+            send_sem=red_s, recv_sem=red_r.at[b, r - 1],
+            device_id=(2 * to + c, d), device_id_type=MESH)
+
+    def half_copy(b, r, half):
+        to = across[r]
+        rows = pl.ds(64 * half, 64)
+        return pltpu.make_async_remote_copy(
+            src_ref=part.at[b, to, rows], dst_ref=got.at[b, r - 1, rows],
             send_sem=red_s, recv_sem=red_r.at[b, r - 1],
             device_id=(2 * to + c, d), device_id_type=MESH)
 
@@ -197,10 +212,11 @@
             total[(c * STEPS + b) * 4 + q] = s[HALF * q:HALF * (q + 1)]
         share_copy(b, c).start()
 
-    def compute(b, kg):
-        for q in range(4):
-            h = q // 2
-            m = b if q % 2 == 0 else 31 - b
+    def compute(b, kg, first, count):
+        for n in range(count):
+            q = first + n
+            h = q % 2
+            m = b if q < 2 else 31 - b
             for p in range(SLOTS):
                 v = held[h, m, kg, p]
                 spread[p] = v
@@ -209,20 +225,19 @@
                 a = tab_s[h, m, kg, 0, 2 * j]
                 e = tab_s[h, m, kg, 0, 2 * j + 1]
                 at = slice(128 * j, 128 * (j + 1))
-                lhs[HALF * q:HALF * q + 16, at] = jnp.where(left, spread[a], spread[VAR + e])
-                lhs[HALF * q + 16:HALF * (q + 1), at] = jnp.where(left, spread[VAR + a], spread[e])
-        prod = jnp.dot(lhs[...], panel[kg], preferred_element_type=jnp.float32)
+                lhs[HALF * n:HALF * n + 16, at] = jnp.where(left, spread[a], spread[VAR + e])
+                lhs[HALF * n + 16:HALF * (n + 1), at] = jnp.where(left, spread[VAR + a], spread[e])
+        prod = jnp.dot(lhs[:HALF * count], panel[kg], preferred_element_type=jnp.float32)
+        at = slice(HALF * first, HALF * (first + count))
         for q in range(4):
             piece = prod[:, 128 * q:128 * (q + 1)]
-            part[b, q] = piece if kg == 0 else part[b, q] + piece
-
-    @pl.loop(0, STEPS)
+            part[b, q, at] = piece if kg == 0 else part[b, q, at] + piece
+
+    @pl.loop(0, STEPS - 1)
     def _(b):
         for h in range(2):
-            @pl.when(b < 15)
-            def _():
-                tab_hop(h, True, b, b + 1).wait_recv()
-                tab_down(h, b + 1).start()
+            tab_hop(h, True, b, b + 1).wait_recv()
+            tab_down(h, b + 1).start()
 
             @pl.when(b < 14)
             def _():
@@ -231,9 +246,7 @@
             tab_hop(h, False, 0, 31 - b).wait_recv()
             tab_down(h, 31 - b).start()
 
-            @pl.when(b < 15)
-            def _():
-                tab_hop(h, False, 31 - b, 30 - b).start()
+            tab_hop(h, False, 31 - b, 30 - b).start()
 
         @pl.when(b == 2)
         def _():
@@ -249,9 +262,7 @@
             for piece in range(CUTS):
                 up_end, down_end = (15, 14) if kg == 0 else (14, 15)
                 for h in range(2):
-                    @pl.when(b < 15)
-                    def _():
-                        hop(h, True, b, b + 1, kg, piece).wait_recv()
+                    hop(h, True, b, b + 1, kg, piece).wait_recv()
 
                     @pl.when(b < up_end)
                     def _():
@@ -269,7 +280,7 @@
                     for h in range(2):
                         tab_down(h, i).wait()
                         tab_down(h, 31 - i).wait()
-                compute(i, kg)
+                compute(i, kg, 0, 4)
                 if kg == 0:
                     @pl.when(i >= 4)
                     def _():
@@ -278,9 +289,31 @@
                     for r in (2, 1, 3):
                         reduce_copy(i, r).start()
 
-    @pl.loop(STEPS - 4, STEPS)
-    def _(b):
-        finish(b)
+    last_b = STEPS - 1
+    for h in range(2):
+        tab_hop(h, False, 0, STEPS).wait_recv()
+        tab_down(h, STEPS).start()
+    for h in range(2):
+        tab_down(h, last_b).wait()
+    for kg in range(2):
+        compute(last_b, kg, 0, 2)
+    for r in (2, 1, 3):
+        half_copy(last_b, r, 0).start()
+    finish(STEPS - 5)
+    finish(STEPS - 4)
+    for h in range(2):
+        tab_down(h, STEPS).wait()
+    for kg in range(2):
+        for piece in range(CUTS):
+            for h in range(2):
+                hop(h, False, 0, STEPS, kg, piece).wait_recv()
+        compute(last_b, kg, 2, 2)
+        if kg == 0:
+            finish(STEPS - 3)
+    for r in (2, 1, 3):
+        half_copy(last_b, r, 1).start()
+    finish(STEPS - 2)
+    finish(STEPS - 1)
 
     @pl.loop(0, STEPS)
     def _(b):
@@ -333,16 +366,20 @@
     lad_n, cyc_n = ladder_count.reshape(2), cycle_count.reshape(2)
 
     hbm = pl.BlockSpec(memory_space=pl.ANY)
-    smem = pl.BlockSpec(memory_space=pltpu.SMEM)
     bf16, f32 = jnp.bfloat16, jnp.float32
     dma = pltpu.SemaphoreType.DMA
     summed = pl.pallas_call(
         kernel,
         name="ladder_ring",
         out_shape=jax.ShapeDtypeStruct((512, 512), f32),
-        in_specs=[hbm] * 2 + [smem] * 5 + [hbm] * 3,
+        in_specs=[hbm] * 10,
         out_specs=pl.BlockSpec(memory_space=pltpu.VMEM),
         scratch_shapes=[
+            pltpu.SMEM((2, KCAP_L), i32),
+            pltpu.SMEM((2,), i32),
+            pltpu.SMEM((2, KCAP_R), i32),
+            pltpu.SMEM((2,), i32),
+            pltpu.SMEM((64,), i32),
             pltpu.VMEM((KCAP_L, 2, TS * TS), bf16),
             pltpu.VMEM((KCAP_R, 2, TS * TS), bf16),
             pltpu.VMEM((2, 2, SLOTS, 16, 128), bf16),
@@ -360,7 +397,7 @@
             pltpu.VMEM((4, 512, 128), f32),
             pltpu.VMEM((3, 512, 128), f32),
             pltpu.VMEM((512, 512), f32),
-            dma((5,)), dma((6,)), dma((6,)), dma((2,)), dma((2, 32)), dma((2, 32)),
+            dma((10,)), dma((6,)), dma((6,)), dma((2,)), dma((2, 32)), dma((2, 32)),
             dma((2,)), dma((2, 32, 2, CUTS)),
             dma, dma((STEPS, 3)), dma, dma((STEPS,)), dma, dma((3,)),
         ],

time: 109 us -> 107 us (0.982)
  Pallas kernels: 107 us -> 105 us
    pallas_call x1, Pallas kernels: 107 us -> 105 us  [per_device(): pl.pallas_call(kernel, name='ladder_ring', out_shape=jax.ShapeDtypeStruct...]
where the time goes in v5:
time: 107 us
  Pallas kernels  105 us (98%)
  local copies, waits for them, and re-layouts  2.26 us (2%)
    pallas_call x1, Pallas kernels, per_device(): pl.pallas_call(kernel, name='ladder_ring', out_shape=jax.ShapeDtypeStruct...  105 us
    unnamed x1, local copies, waits for them, and re-layouts  2.26 us

profile of v5, /device:TPU:1, one launch (start us, length us, event | category | flops | bytes accessed | tf_op | source)
XLA Modules:
  0.0 106.8 jit_solution(13033839029240372116)
XLA Ops:
  0.0 104.5 %ladder_ring.1 = f32[512,512]{1,0:T(8,128)} custom-call(bf16[18,2,4096]{2,1,0:T(2,128)(2,1)} %bitcast.4, bf16[6,2,4096]{2,1,0:T(2,128)(2,1)} %bitcast.5, s32[2,18]{1,0:T(2,128)} %lad_ids_h.1, s32[2]{0:T(128)} %bitcast.6, s32[2,6]{1,0:T(2,128)} %cyc_ids_h.1, s32[2]{0:T(128)} %bitcast.7, s32[64]{0:T(128)} %owners_h.1, bf16[1536,512]{1,0:T(8,128)(2,1)} %lad.1, ...), custom_call_target="tpu_custom_call" | custom-call | tf_op jit(solution)/shard_map/ladder_ring/pallas_call | solution.py:371
  104.6 2.3 %copy.12 = f32[512,512]{1,0:T(8,128)} copy(f32[512,512]{1,0:T(8,128)} %ladder_ring.1) | data formatting | bytes 2097152

commit v6 on v5

--- a/solution.py
+++ b/solution.py
@@ -286,7 +286,7 @@
                     def _():
                         finish(i - 4)
                 else:
-                    for r in (2, 1, 3):
+                    for r in (1, 3, 2):
                         reduce_copy(i, r).start()
 
     last_b = STEPS - 1
@@ -297,7 +297,7 @@
         tab_down(h, last_b).wait()
     for kg in range(2):
         compute(last_b, kg, 0, 2)
-    for r in (2, 1, 3):
+    for r in (1, 3, 2):
         half_copy(last_b, r, 0).start()
     finish(STEPS - 5)
     finish(STEPS - 4)
@@ -310,7 +310,7 @@
         compute(last_b, kg, 2, 2)
         if kg == 0:
             finish(STEPS - 3)
-    for r in (2, 1, 3):
+    for r in (1, 3, 2):
         half_copy(last_b, r, 1).start()
     finish(STEPS - 2)
     finish(STEPS - 1)

time: 107 us -> 107 us (level)
  no operation moved by 1% of the time
where the time goes in v6:
time: 107 us
  Pallas kernels  105 us (98%)
  local copies, waits for them, and re-layouts  2.26 us (2%)
    pallas_call x1, Pallas kernels, per_device(): pl.pallas_call(kernel, name='ladder_ring', out_shape=jax.ShapeDtypeStruct...  105 us
    unnamed x1, local copies, waits for them, and re-layouts  2.26 us

profile of v6, /device:TPU:1, one launch (start us, length us, event | category | flops | bytes accessed | tf_op | source)
XLA Modules:
  0.0 106.9 jit_solution(6186822873842307164)
XLA Ops:
  0.0 104.6 %ladder_ring.1 = f32[512,512]{1,0:T(8,128)} custom-call(bf16[18,2,4096]{2,1,0:T(2,128)(2,1)} %bitcast.4, bf16[6,2,4096]{2,1,0:T(2,128)(2,1)} %bitcast.5, s32[2,18]{1,0:T(2,128)} %lad_ids_h.1, s32[2]{0:T(128)} %bitcast.6, s32[2,6]{1,0:T(2,128)} %cyc_ids_h.1, s32[2]{0:T(128)} %bitcast.7, s32[64]{0:T(128)} %owners_h.1, bf16[1536,512]{1,0:T(8,128)(2,1)} %lad.1, ...), custom_call_target="tpu_custom_call" | custom-call | tf_op jit(solution)/shard_map/ladder_ring/pallas_call | solution.py:371
  104.6 2.3 %copy.12 = f32[512,512]{1,0:T(8,128)} copy(f32[512,512]{1,0:T(8,128)} %ladder_ring.1) | data formatting | bytes 2097152
